TPU v7x, 32 devices: a whole 2x2x4 slice. The times are simulated.
32 devices in a mesh: wide: 16 (over z, y, x), narrow: 2 (over core).
Axes of the slice: x: 2, y: 2, z: 4, core: 2. Of those that a mesh axis runs over, the one named last changes fastest.
Arguments:
- grads: bfloat16 [14, 512, 2048], P(None, 'wide', 'narrow'), may hold values from -200 to 200
- momentum: float32 [14, 512, 2048], P(None, 'wide', 'narrow'), may hold values from -400 to 400
- owners: int32 [14], replicated, may hold values from 0 to 15, as said below
- norm_grads: float32 [28, 2048], P('narrow', 'wide'), may hold values from -6 to 6
- norm_params: float32 [28, 2048], P('narrow', 'wide'), may hold values from 0.5 to 1.5
- adam_m: float32 [28, 2048], P('narrow', 'wide'), may hold values from -4 to 4
- adam_v: float32 [28, 2048], P('narrow', 'wide'), may hold values from 0.1 to 4
Outputs:
- muon_update: bfloat16 [14, 512, 2048], P(None, 'wide', 'narrow')
- momentum_new: float32 [14, 512, 2048], P(None, 'wide', 'narrow')
- owner_load: float32 [16], P('wide')
- norm_params_new: float32 [28, 2048], P('narrow', 'wide')
- adam_m_new: float32 [28, 2048], P('narrow', 'wide')
- adam_v_new: float32 [28, 2048], P('narrow', 'wide')
Inputs may be any that keep to these rules, and one draw needn't show every extreme that they name: `owners`: each of the 16 groups owns at most 2 matrices, and some group owns exactly 2.
All inputs are finite; a program needn't handle non-finite values.
Results may differ from a plain program's by a relative error of at most 0.014.
Values may be sent and summed in bfloat16 or wider, within the bound.
A program may use at most 64 MiB of HBM per device.

v0:
```python
import math
import jax
import jax.numpy as jnp
from jax import lax
from jax.sharding import PartitionSpec as P

D = 2048
KV_OUT = 512
ITERS = 2
coef_a = 3.4445
coef_b = -4.775
coef_c = 2.0315
muon_beta = 0.95
norm_eps = 1e-07
adam_first = 0.9
adam_second = 0.95
adam_rate = 0.02
adam_eps = 1e-08
first_fix = 1.0 - 0.9**10
second_fix = 1.0 - 0.95**10


def polynomial_times(current, partial_value):
    gram_sum = lax.psum(partial_value.astype(jnp.bfloat16), "narrow")
    square = jnp.einsum("cmk,ckn->cmn", gram_sum, gram_sum, preferred_element_type=jnp.float32)
    polynomial = (coef_b * gram_sum.astype(jnp.float32) + coef_c * square).astype(jnp.bfloat16)
    return jnp.einsum("cmk,ckn->cmn", polynomial, current, preferred_element_type=jnp.float32)


def newton_schulz(current):
    result = current.astype(jnp.float32)
    for iteration in range(ITERS):
        partial_value = jnp.einsum(
            "cmk,cnk->cmn", current, current, preferred_element_type=jnp.float32
        )
        product_bx = polynomial_times(current, partial_value)
        result = coef_a * current.astype(jnp.float32) + product_bx
        if iteration + 1 < ITERS:
            current = result.astype(jnp.bfloat16)
    updates = (math.sqrt(D) * result).astype(jnp.bfloat16)
    update_values = updates.astype(jnp.float32)
    update_squares = lax.psum(jnp.sum(update_values * update_values, axis=(1, 2)), "narrow")
    return (updates[None], (update_squares / (KV_OUT * D))[None])


def orthogonalize(slot_block):
    directions = slot_block[0]
    square_sums = lax.psum(jnp.sum(directions * directions, axis=(1, 2)), "narrow")
    current = (directions / (jnp.sqrt(square_sums)[:, None, None] + norm_eps)).astype(jnp.bfloat16)
    return newton_schulz(current)


def on_device(grads, momentum, owners, norm_grads, norm_params, adam_m, adam_v):
    grad_values = grads.astype(jnp.float32)
    momentum_new = muon_beta * momentum + grad_values
    direction = grad_values + muon_beta * momentum_new
    groups = lax.axis_size("wide")
    matrix_count = owners.shape[0]
    matrix_ids = jnp.arange(matrix_count, dtype=jnp.int32)
    capacity = -(-matrix_count // groups)
    slot_of = matrix_ids % groups * capacity + matrix_ids // groups
    slot_total = groups * capacity
    slot_match = slot_of[None, :] == jnp.arange(slot_total, dtype=jnp.int32)[:, None]
    source = jnp.sum(jnp.where(slot_match, matrix_ids[None, :], 0), axis=1) + jnp.where(
        jnp.any(slot_match, axis=1), 0, matrix_count
    )
    row_count = direction.shape[1]
    col_count = direction.shape[2]
    padded = jnp.concatenate([direction, jnp.zeros((1, row_count, col_count), jnp.float32)], axis=0)
    outgoing = jnp.take(padded, source, axis=0).reshape(groups, capacity, row_count, col_count)
    updates, slot_loads = orthogonalize(
        lax.all_to_all(outgoing, "wide", split_axis=0, concat_axis=2, tiled=True)
    )
    returned = lax.all_to_all(updates, "wide", split_axis=2, concat_axis=0, tiled=True)
    arrived = returned.reshape(slot_total, row_count, col_count)
    muon_update = jnp.take(arrived, slot_of, axis=0)
    own_group = lax.axis_index("wide")
    computed_here = matrix_ids % groups == own_group
    local_loads = jnp.where(computed_here, jnp.take(slot_loads[0], matrix_ids // groups), 0.0)
    matrix_loads = lax.psum(local_loads, "wide")
    owner_load = jnp.sum(jnp.where(owners == own_group, matrix_loads, 0.0)).reshape(1)
    adam_m_new = adam_first * adam_m + (1.0 - adam_first) * norm_grads
    adam_v_new = adam_second * adam_v + (1.0 - adam_second) * norm_grads * norm_grads
    corrected = adam_m_new / first_fix / (jnp.sqrt(adam_v_new / second_fix) + adam_eps)
    norm_params_new = norm_params - adam_rate * corrected
    return (muon_update, momentum_new, owner_load, norm_params_new, adam_m_new, adam_v_new)


def solution(mesh):
    return jax.shard_map(
        on_device,
        mesh=mesh,
        in_specs=(
            P(None, "wide", "narrow"),
            P(None, "wide", "narrow"),
            P(),
            P("narrow", "wide"),
            P("narrow", "wide"),
            P("narrow", "wide"),
            P("narrow", "wide"),
        ),
        out_specs=(
            P(None, "wide", "narrow"),
            P(None, "wide", "narrow"),
            P("wide"),
            P("narrow", "wide"),
            P("narrow", "wide"),
            P("narrow", "wide"),
        ),
        check_vma=False,
    )
```

profile of v0, /device:TPU:0, one launch (start us, length us, event | category | flops | bytes accessed | tf_op | source)
XLA Modules:
  0.0 207.1 jit_solution(12475647661025235217)
XLA Ops:
  7.2 0.0 all-reduce.4.cloned.1.call-start
  7.2 0.1 fusion.20
  7.3 0.1 select_reduce_fusion
  7.5 3.5 %convert_add_fusion = (f32[14,32,1024]{2,1,0:T(8,128)S(1)}, f32[14,32,1024]{2,1,0:T(8,128)}) fusion(bf16[14,32,1024]{2,1,0:T(8,128)(2,1)} %param.7, f32[14,32,1024]{2,1,0:T(8,128)} %param.8), kind=kLoop, calls=%fused_computation.2 | loop fusion | flops 2293760 | bytes 6422528 | tf_op jit(solution)/shard_map/add | solution.py:56
  11.0 0.3 concatenate.3
  11.2 2.0 gather_fusion
  13.3 1.8 bitcast_select_fusion
  15.1 57.0 %all_to_all.8 = f32[16,1,32,1024]{3,2,1,0:T(8,128)S(1)} all-to-all(f32[16,1,32,1024]{3,2,1,0:T(8,128)S(1)} %bitcast_select_fusion), channel_id=1, replica_groups=mesh['wide'=16,'narrow'=2] {'wide'}, dimensions={0} | all-to-all | bytes 4194304 | tf_op jit(solution)/shard_map/all_to_all | solution.py:72
  72.1 1.1 multiply_reduce_fusion.1
  73.2 3.1 %psum.35 = f32[1]{0:T(128)} all-reduce(f32[1]{0:T(128)} %bitcast.3), channel_id=1, replica_groups=mesh['wide'=16,'narrow'=2] {'narrow'}, use_global_device_ids=true, to_apply=%region_3.4 | all-reduce | flops 1 | bytes 8 | tf_op jit(solution)/shard_map/psum | solution.py:48
  77.0 1.7 convert_multiply_fusion
  78.7 0.0 copy-start
  78.7 1.5 fusion.7
  80.2 0.0 all-reduce.4.cloned.1.call-update
  80.3 0.2 all-reduce.6.cloned.1.call-start
  80.5 16.9 %all-reduce.4.cloned.1.call-done = bf16[1,512,512]{2,1,0:T(8,128)(2,1)} async-done(((bf16[1,512,512]{2,1,0:T(8,128)(2,1)}), bf16[1,512,512]{2,1,0:T(8,128)(2,1)}) %all-reduce.4.cloned.1.call-update) | async-done | bytes 524304 | tf_op jit(solution)/shard_map/psum | solution.py:24
  97.4 0.0 copy-done
  97.4 3.4 %fusion = bf16[512,1024]{1,0:T(8,128)(2,1)} fusion(f32[16,1,32,1024]{3,2,1,0:T(8,128)S(1)} %copy-done, bf16[512,1024]{1,0:T(8,128)(2,1)S(1)} %bitcast.81, bf16[1,512,512]{2,1,0:T(8,128)(2,1)} %all-reduce.4.cloned.1.call-done), kind=kOutput, calls=%fused_computation.5 | convolution fusion | flops 807665664 | bytes 4718592 | tf_op jit(solution)/shard_map/cmk,ckn->cmn/dot_general | solution.py:27
  100.8 0.0 copy-start.6
  100.8 3.2 %fusion.8 = bf16[1,512,512]{2,1,0:T(8,128)(2,1)} fusion(bf16[512,1024]{1,0:T(8,128)(2,1)} %fusion), kind=kOutput, calls=%fused_computation.23 | convolution fusion | flops 537133056 | bytes 1572864 | tf_op jit(solution)/shard_map/cmk,cnk->cmn/dot_general | solution.py:33
  104.0 0.0 all-reduce.6.cloned.1.call-update
  104.0 20.1 %all-reduce.6.cloned.1.call-done = bf16[1,512,512]{2,1,0:T(8,128)(2,1)} async-done(((bf16[1,512,512]{2,1,0:T(8,128)(2,1)}), bf16[1,512,512]{2,1,0:T(8,128)(2,1)}) %all-reduce.6.cloned.1.call-update) | async-done | bytes 524304 | tf_op jit(solution)/shard_map/psum | solution.py:24
  124.1 0.0 copy-done.6
  124.1 3.2 %multiply_reduce_fusion = (f32[]{:T(128)}, bf16[512,1024]{1,0:T(8,128)(2,1)S(1)}) fusion(bf16[512,1024]{1,0:T(8,128)(2,1)S(1)} %copy-done.6, bf16[1,512,512]{2,1,0:T(8,128)(2,1)} %all-reduce.6.cloned.1.call-done), kind=kOutput, calls=%fused_computation.7 | convolution fusion | flops 810811392 | bytes 2621444 | tf_op jit(solution)/shard_map/cmk,ckn->cmn/dot_general | solution.py:27
  127.3 1.6 copy.18
  128.9 0.5 broadcast.355
  129.5 6.8 %reduce.3 = bf16[512,1024]{1,0:T(8,128)(2,1)S(1)} reduce(bf16[512,1,1,1024]{3,2,1,0:T(2,128)(2,1)S(1)} %bitcast.77, bf16[]{:T(256)} %broadcast.355), dimensions={1,2}, to_apply=%bitcast.75.reduce_sub_computation | reduce | bytes 2097154
  136.2 0.0 copy-start.1
  136.3 0.0 copy-start.2
  136.3 0.0 copy-start.3
  136.3 0.0 copy-start.4
  136.3 0.0 copy-start.5
  136.3 1.6 reshape.253
  137.9 6.8 %all-to-all-start.1 = ((bf16[16,2,16384]{2,1,0:T(2,128)(2,1)}), bf16[16,2,16384]{2,1,0:T(2,128)(2,1)S(1)}, u32[]{:S(2)}, u32[]{:S(2)}) async-start(bf16[16,2,16384]{2,1,0:T(2,128)(2,1)} %reshape.253), calls=%async_computation.1 | async-start | bytes 2097152 | tf_op jit(solution)/shard_map/all_to_all | solution.py:74
  144.7 0.0 copy-done.1
  144.8 0.0 copy-done.2
  144.8 0.0 copy-done.3
  144.8 0.0 copy-done.4
  144.8 0.6 multiply_subtract_fusion
  145.4 3.1 %psum.38 = f32[1]{0:T(128)} all-reduce(f32[1]{0:T(128)} %bitcast.17), channel_id=1, replica_groups=mesh['wide'=16,'narrow'=2] {'narrow'}, use_global_device_ids=true, to_apply=%region_7.8 | all-reduce | flops 1 | bytes 8 | tf_op jit(solution)/shard_map/psum | solution.py:42
  149.2 47.4 %psum.39 = f32[14]{0:T(128)S(1)} all-reduce(f32[14]{0:T(128)S(1)} %compare_select_fusion.5), channel_id=1, replica_groups=mesh['wide'=16,'narrow'=2] {'wide'}, use_global_device_ids=true, to_apply=%region_8.9 | all-reduce | flops 14 | bytes 112 | tf_op jit(solution)/shard_map/psum | solution.py:80
  196.6 0.0 copy-done.5
  196.6 0.6 fusion.23
  197.2 0.0 all-to-all-done.1
  197.2 1.0 reshape.254
  198.2 0.4 copy.16
  198.6 0.6 gather_fusion.1
  199.2 1.1 broadcast_select_fusion
  (8 shorter events, 0.1 us)
Async XLA Ops:
  7.2 90.2 %all-reduce.4.cloned.1.call-start = ((), (), s32[]{:S(2)}) async-start(), calls=%async_computation.2 | async-start | bytes 1048576 | tf_op jit(solution)/shard_map/psum | solution.py:24
  78.7 18.7 %copy-start = (f32[16,1,32,1024]{3,2,1,0:T(8,128)S(1)}, f32[16,1,32,1024]{3,2,1,0:T(8,128)}, u32[]{:S(2)}) copy-start(f32[16,1,32,1024]{3,2,1,0:T(8,128)} %get-tuple-element.9) | copy-start | bytes 6291460
  80.3 43.8 %all-reduce.6.cloned.1.call-start = ((), (), s32[]{:S(2)}) async-start(), calls=%async_computation.3 | async-start | bytes 1048576 | tf_op jit(solution)/shard_map/psum | solution.py:24
  100.8 23.3 %copy-start.6 = (bf16[512,1024]{1,0:T(8,128)(2,1)S(1)}, bf16[512,1024]{1,0:T(8,128)(2,1)}, u32[]{:S(2)}) copy-start(bf16[512,1024]{1,0:T(8,128)(2,1)} %fusion) | copy-start | bytes 3145732
  136.2 8.5 %copy-start.1 = (f32[14,128]{1,0:T(8,128)S(1)}, f32[14,128]{1,0:T(8,128)}, u32[]{:S(2)}) copy-start(f32[14,128]{1,0:T(8,128)} %param.11) | copy-start | bytes 21508
  136.3 8.5 %copy-start.2 = (f32[14,128]{1,0:T(8,128)S(1)}, f32[14,128]{1,0:T(8,128)}, u32[]{:S(2)}) copy-start(f32[14,128]{1,0:T(8,128)} %param.10) | copy-start | bytes 21508
  136.3 8.5 %copy-start.3 = (f32[14,128]{1,0:T(8,128)S(1)}, f32[14,128]{1,0:T(8,128)}, u32[]{:S(2)}) copy-start(f32[14,128]{1,0:T(8,128)} %param.12) | copy-start | bytes 21508
  136.3 8.5 %copy-start.4 = (f32[14,128]{1,0:T(8,128)S(1)}, f32[14,128]{1,0:T(8,128)}, u32[]{:S(2)}) copy-start(f32[14,128]{1,0:T(8,128)} %param.13) | copy-start | bytes 21508
  136.3 60.3 %copy-start.5 = (s32[14]{0:T(128)S(1)}, s32[14]{0:T(128)}, u32[]{:S(2)}) copy-start(s32[14]{0:T(128)} %param.9) | copy-start | bytes 172
  137.9 59.3 %all-to-all-start.1 = ((bf16[16,2,16384]{2,1,0:T(2,128)(2,1)}), bf16[16,2,16384]{2,1,0:T(2,128)(2,1)S(1)}, u32[]{:S(2)}, u32[]{:S(2)}) async-start(bf16[16,2,16384]{2,1,0:T(2,128)(2,1)} %reshape.253), calls=%async_computation.1 | async-start | bytes 2097152 | tf_op jit(solution)/shard_map/all_to_all | solution.py:74
Sparse Core Ops, SparseCore 0:
  80.4 16.9 all-reduce.3
  104.1 19.9 all-reduce.5
where the time goes:
time: 208 us; the launch traced here: 207 us
  blocking collectives  111 us (53%)
  waiting for transfers between devices  37 us (18%)
  other arithmetic  17.5 us (8%)
  between operations  15.6 us (8%)
  matrix products  11.3 us (5%)
  local copies, waits for them, and re-layouts  8.1 us (4%)
  starting transfers between devices  7.05 us (3%)
    all_to_all x1, blocking collectives, on_device(): lax.all_to_all(outgoing, 'wide', split_axis=0, concat_axis=2, tiled=True)  57 us
    psum x1, blocking collectives, on_device(): matrix_loads = lax.psum(local_loads, 'wide')  47.4 us
    psum x2, waiting for transfers between devices, polynomial_times(): gram_sum = lax.psum(partial_value.astype(jnp.bfloat16), 'narrow')  37 us
    all_to_all x1, starting transfers between devices, on_device(): lax.all_to_all(updates, 'wide', split_axis=2, concat_axis=0, tiled=True)  6.79 us
    unnamed x1, other arithmetic  6.78 us
    dot_general x2, matrix products, polynomial_times(): jnp.einsum('cmk,ckn->cmn', polynomial, current, preferred_element_type=jn...  6.64 us
    dot_general x2, matrix products, newton_schulz(): jnp.einsum('cmk,cnk->cmn', current, current, preferred_element_type=jnp.f...  4.71 us
  transfers between devices with their start and end apart: 3, of which 2 were waited for; matrix products, arithmetic and copies ran while one was open for 1% of the time, Pallas kernels for 0%

commit v1 on v0

--- a/solution.py
+++ b/solution.py
@@ -71,7 +71,9 @@
     updates, slot_loads = orthogonalize(
         lax.all_to_all(outgoing, "wide", split_axis=0, concat_axis=2, tiled=True)
     )
-    returned = lax.all_to_all(updates, "wide", split_axis=2, concat_axis=0, tiled=True)
+    returned = jnp.concatenate(
+        lax.all_to_all(jnp.stack(jnp.split(updates, lax.axis_size("wide"), 2), 0), "wide", 0, 0), 0
+    )
     arrived = returned.reshape(slot_total, row_count, col_count)
     muon_update = jnp.take(arrived, slot_of, axis=0)
     own_group = lax.axis_index("wide")

time: 208 us -> 206 us (level)
  other arithmetic: 17.5 us -> 10.7 us
  local copies, waits for them, and re-layouts: 8.1 us -> 12.9 us
    unnamed x1 -> x0, other arithmetic: 6.78 us -> none
    unnamed x18 -> x29, local copies, waits for them, and re-layouts: 3.57 us -> 9.37 us
where the time goes in v1:
time: 206 us; the launch traced here: 205 us
  blocking collectives  111 us (54%)
  waiting for transfers between devices  37.2 us (18%)
  between operations  15.5 us (8%)
  local copies, waits for them, and re-layouts  12.9 us (6%)
  matrix products  11.4 us (6%)
  other arithmetic  10.7 us (5%)
  starting transfers between devices  6.87 us (3%)
    all_to_all x1, blocking collectives, on_device(): lax.all_to_all(outgoing, 'wide', split_axis=0, concat_axis=2, tiled=True)  57 us
    psum x1, blocking collectives, on_device(): matrix_loads = lax.psum(local_loads, 'wide')  47.4 us
    psum x2, waiting for transfers between devices, polynomial_times(): gram_sum = lax.psum(partial_value.astype(jnp.bfloat16), 'narrow')  37.2 us
    unnamed x29, local copies, waits for them, and re-layouts  9.37 us
    all_to_all x1, starting transfers between devices, on_device(): lax.all_to_all(jnp.stack(jnp.split(updates, lax.axis_size('wide'), 2), 0)...  6.79 us
    dot_general x2, matrix products, polynomial_times(): jnp.einsum('cmk,ckn->cmn', polynomial, current, preferred_element_type=jn...  6.71 us
    dot_general x2, matrix products, newton_schulz(): jnp.einsum('cmk,cnk->cmn', current, current, preferred_element_type=jnp.f...  4.7 us
  transfers between devices with their start and end apart: 3, of which 2 were waited for; matrix products, arithmetic and copies ran while one was open for 1% of the time, Pallas kernels for 0%

profile of v1, /device:TPU:0, one launch (start us, length us, event | category | flops | bytes accessed | tf_op | source)
XLA Modules:
  0.0 205.2 jit_solution(14227385031190158238)
XLA Ops:
  7.2 0.0 all-reduce.4.cloned.1.call-start
  7.2 0.1 fusion.36
  7.3 0.1 select_reduce_fusion
  7.5 3.5 %convert_add_fusion = (f32[14,32,1024]{2,1,0:T(8,128)S(1)}, f32[14,32,1024]{2,1,0:T(8,128)}) fusion(bf16[14,32,1024]{2,1,0:T(8,128)(2,1)} %param.7, f32[14,32,1024]{2,1,0:T(8,128)} %param.8), kind=kLoop, calls=%fused_computation.2 | loop fusion | flops 2293760 | bytes 6422528 | tf_op jit(solution)/shard_map/add | solution.py:56
  11.0 0.3 concatenate.3
  11.2 2.0 gather_fusion
  13.3 1.8 bitcast_select_fusion
  15.1 57.0 %all_to_all.14 = f32[16,1,32,1024]{3,2,1,0:T(8,128)S(1)} all-to-all(f32[16,1,32,1024]{3,2,1,0:T(8,128)S(1)} %bitcast_select_fusion), channel_id=1, replica_groups=mesh['wide'=16,'narrow'=2] {'wide'}, dimensions={0} | all-to-all | bytes 4194304 | tf_op jit(solution)/shard_map/all_to_all | solution.py:72
  72.1 1.1 multiply_reduce_fusion.1
  73.2 3.1 %psum.35 = f32[1]{0:T(128)} all-reduce(f32[1]{0:T(128)} %bitcast.3), channel_id=1, replica_groups=mesh['wide'=16,'narrow'=2] {'narrow'}, use_global_device_ids=true, to_apply=%region_3.4 | all-reduce | flops 1 | bytes 8 | tf_op jit(solution)/shard_map/psum | solution.py:48
  77.0 1.7 convert_multiply_fusion
  78.7 0.0 copy-start
  78.7 1.5 fusion.7
  80.2 0.0 all-reduce.4.cloned.1.call-update
  80.3 0.0 all-reduce.6.cloned.1.call-start
  80.3 17.1 %all-reduce.4.cloned.1.call-done = bf16[1,512,512]{2,1,0:T(8,128)(2,1)} async-done(((bf16[1,512,512]{2,1,0:T(8,128)(2,1)}), bf16[1,512,512]{2,1,0:T(8,128)(2,1)}) %all-reduce.4.cloned.1.call-update) | async-done | bytes 524304 | tf_op jit(solution)/shard_map/psum | solution.py:24
  97.4 0.0 copy-done
  97.4 3.4 %fusion = bf16[512,1024]{1,0:T(8,128)(2,1)} fusion(f32[16,1,32,1024]{3,2,1,0:T(8,128)S(1)} %copy-done, bf16[512,1024]{1,0:T(8,128)(2,1)S(1)} %bitcast.154, bf16[1,512,512]{2,1,0:T(8,128)(2,1)} %all-reduce.4.cloned.1.call-done), kind=kOutput, calls=%fused_computation.5 | convolution fusion | flops 807665664 | bytes 4718592 | tf_op jit(solution)/shard_map/cmk,ckn->cmn/dot_general | solution.py:27
  100.8 0.0 copy-start.6
  100.8 3.2 %fusion.8 = bf16[1,512,512]{2,1,0:T(8,128)(2,1)} fusion(bf16[512,1024]{1,0:T(8,128)(2,1)} %fusion), kind=kOutput, calls=%fused_computation.23 | convolution fusion | flops 537133056 | bytes 1572864 | tf_op jit(solution)/shard_map/cmk,cnk->cmn/dot_general | solution.py:33
  104.0 0.0 all-reduce.6.cloned.1.call-update
  104.0 20.1 %all-reduce.6.cloned.1.call-done = bf16[1,512,512]{2,1,0:T(8,128)(2,1)} async-done(((bf16[1,512,512]{2,1,0:T(8,128)(2,1)}), bf16[1,512,512]{2,1,0:T(8,128)(2,1)}) %all-reduce.6.cloned.1.call-update) | async-done | bytes 524304 | tf_op jit(solution)/shard_map/psum | solution.py:24
  124.1 0.0 copy-done.6
  124.1 3.3 %multiply_reduce_fusion = (f32[]{:T(128)}, bf16[512,1024]{1,0:T(8,128)(2,1)S(1)}) fusion(bf16[512,1024]{1,0:T(8,128)(2,1)S(1)} %copy-done.6, bf16[1,512,512]{2,1,0:T(8,128)(2,1)} %all-reduce.6.cloned.1.call-done), kind=kOutput, calls=%fused_computation.7 | convolution fusion | flops 810811392 | bytes 2621444 | tf_op jit(solution)/shard_map/cmk,ckn->cmn/dot_general | solution.py:27
  127.4 0.0 copy-start.1
  127.4 0.0 copy-start.2
  127.4 0.0 copy-start.3
  127.4 0.0 copy-start.4
  127.4 0.6 fusion.34
  128.0 0.0 copy-start.5
  128.0 0.6 fusion.33
  128.6 0.6 fusion.32
  129.3 0.6 fusion.31
  129.9 0.6 fusion.30
  130.5 0.6 fusion.29
  131.1 0.6 fusion.28
  131.8 0.6 fusion.27
  132.4 0.6 fusion.26
  133.0 0.6 fusion.25
  133.6 0.6 fusion.24
  134.2 0.6 fusion.23
  134.9 0.6 fusion.22
  135.5 0.6 fusion.21
  136.1 0.6 fusion.20
  136.7 0.6 fusion.19
  137.4 6.8 %all-to-all-start.1 = ((bf16[16,1,1,32,1024]{4,3,2,1,0:T(8,128)(2,1)}), bf16[16,1,1,32,1024]{4,3,2,1,0:T(8,128)(2,1)S(1)}, u32[]{:S(2)}, u32[]{:S(2)}) async-start(bf16[16,1,1,32,1024]{4,3,2,1,0:T(8,128)(2,1)} %fusion.19), calls=%async_computation.1 | async-start | bytes 2097152 | tf_op jit(solution)/shard_map/all_to_all | solution.py:75
  144.2 0.0 copy-done.1
  144.2 0.0 copy-done.2
  144.2 0.0 copy-done.3
  144.2 0.0 copy-done.4
  144.3 0.6 multiply_subtract_fusion
  144.9 3.1 %psum.38 = f32[1]{0:T(128)} all-reduce(f32[1]{0:T(128)} %bitcast.34), channel_id=1, replica_groups=mesh['wide'=16,'narrow'=2] {'narrow'}, use_global_device_ids=true, to_apply=%region_7.8 | all-reduce | flops 1 | bytes 8 | tf_op jit(solution)/shard_map/psum | solution.py:42
  148.6 47.4 %psum.39 = f32[14]{0:T(128)S(1)} all-reduce(f32[14]{0:T(128)S(1)} %compare_select_fusion.5), channel_id=1, replica_groups=mesh['wide'=16,'narrow'=2] {'wide'}, use_global_device_ids=true, to_apply=%region_8.9 | all-reduce | flops 14 | bytes 112 | tf_op jit(solution)/shard_map/psum | solution.py:82
  196.0 0.0 copy-done.5
  196.0 0.6 fusion.39
  196.6 0.0 all-to-all-done.1
  196.7 0.6 gather_fusion.1
  197.3 1.1 broadcast_select_fusion
  (8 shorter events, 0.1 us)
Async XLA Ops:
  7.2 90.2 %all-reduce.4.cloned.1.call-start = ((), (), s32[]{:S(2)}) async-start(), calls=%async_computation.2 | async-start | bytes 1048576 | tf_op jit(solution)/shard_map/psum | solution.py:24
  78.7 18.7 %copy-start = (f32[16,1,32,1024]{3,2,1,0:T(8,128)S(1)}, f32[16,1,32,1024]{3,2,1,0:T(8,128)}, u32[]{:S(2)}) copy-start(f32[16,1,32,1024]{3,2,1,0:T(8,128)} %get-tuple-element.9) | copy-start | bytes 6291460
  80.3 43.8 %all-reduce.6.cloned.1.call-start = ((), (), s32[]{:S(2)}) async-start(), calls=%async_computation.3 | async-start | bytes 1048576 | tf_op jit(solution)/shard_map/psum | solution.py:24
  100.8 23.3 %copy-start.6 = (bf16[512,1024]{1,0:T(8,128)(2,1)S(1)}, bf16[512,1024]{1,0:T(8,128)(2,1)}, u32[]{:S(2)}) copy-start(bf16[512,1024]{1,0:T(8,128)(2,1)} %fusion) | copy-start | bytes 3145732
  127.4 16.8 %copy-start.1 = (f32[14,128]{1,0:T(8,128)S(1)}, f32[14,128]{1,0:T(8,128)}, u32[]{:S(2)}) copy-start(f32[14,128]{1,0:T(8,128)} %param.11) | copy-start | bytes 21508
  127.4 16.9 %copy-start.2 = (f32[14,128]{1,0:T(8,128)S(1)}, f32[14,128]{1,0:T(8,128)}, u32[]{:S(2)}) copy-start(f32[14,128]{1,0:T(8,128)} %param.10) | copy-start | bytes 21508
  127.4 16.9 %copy-start.3 = (f32[14,128]{1,0:T(8,128)S(1)}, f32[14,128]{1,0:T(8,128)}, u32[]{:S(2)}) copy-start(f32[14,128]{1,0:T(8,128)} %param.12) | copy-start | bytes 21508
  127.4 16.9 %copy-start.4 = (f32[14,128]{1,0:T(8,128)S(1)}, f32[14,128]{1,0:T(8,128)}, u32[]{:S(2)}) copy-start(f32[14,128]{1,0:T(8,128)} %param.13) | copy-start | bytes 21508
  128.0 68.0 %copy-start.5 = (s32[14]{0:T(128)S(1)}, s32[14]{0:T(128)}, u32[]{:S(2)}) copy-start(s32[14]{0:T(128)} %param.9) | copy-start | bytes 172
  137.4 59.3 %all-to-all-start.1 = ((bf16[16,1,1,32,1024]{4,3,2,1,0:T(8,128)(2,1)}), bf16[16,1,1,32,1024]{4,3,2,1,0:T(8,128)(2,1)S(1)}, u32[]{:S(2)}, u32[]{:S(2)}) async-start(bf16[16,1,1,32,1024]{4,3,2,1,0:T(8,128)(2,1)} %fusion.19), calls=%async_computation.1 | async-start | bytes 2097152 | tf_op jit(solution)/shard_map/all_to_all | solution.py:75
Sparse Core Ops, SparseCore 0:
  80.4 16.9 all-reduce.3
  104.1 19.8 all-reduce.5
